TPU v7x, 512 devices: a whole 4x4x16 slice. The times are simulated.
512 devices in a mesh: ctx: 16 (over y, z_lo), exp: 32 (over z_hi, x, core).
Axes of the slice: x: 4, y: 4, z: 16 (z_hi: 4, z_lo: 4; z = z_hi * 4 + z_lo), core: 2. Of those that a mesh axis runs over, the one named last changes fastest.
Arguments:
- query: bfloat16 [32, 1024, 2048], P('exp', 'ctx'), may hold values from -24 to 24
- key_value: bfloat16 [32, 1024, 2, 256], P('exp', 'ctx'), may hold values from -24 to 24
- positions: int32 [32, 1024], P('exp', 'ctx'), may hold values from 0 to 1023, as said below
- resid: bfloat16 [32, 1024, 1440], P('exp', 'ctx'), may hold values from -6 to 6
- sinks: float32 [32], replicated, may hold values from -2 to 3
- o_weight: bfloat16 [2048, 1440], P('exp'), may hold values from -0.125 to 0.125
- norm_gain: float32 [1440], replicated, may hold values from 0.25 to 1.75
- expert_ids: int32 [32, 1024, 4], P('exp', 'ctx'), may hold values from 0 to 127, all different within a row; in each aligned block of 64 rows (0 to 63, 64 to 127, ..., all dimensions but the last counted through in order) at most 2 rows name the same one
- route_weights: float32 [32, 1024, 4], P('exp', 'ctx'), may hold values from 0.1 to 0.5
- w_gate: bfloat16 [1440, 184320], P(None, ('ctx', 'exp')), may hold values from -0.15625 to 0.15625
- w_up: bfloat16 [1440, 184320], P(None, ('ctx', 'exp')), may hold values from -0.15625 to 0.15625
- w_down: bfloat16 [184320, 1440], P(('ctx', 'exp')), may hold values from -0.15625 to 0.15625
Outputs:
- out: bfloat16 [32, 1024, 1440], P('exp', 'ctx')
Inputs may be any that keep to these rules, and one draw needn't show every extreme that they name: Within each sequence every position appears once; the 64 stored rows of one device are two runs of 32 consecutive ascending positions, each run starting at a multiple of 32. `expert_ids`: each row names 4 different experts; among the 64 rows of one device no expert is named more than 2 times, a bound that some block reaches.
All inputs are finite; a program needn't handle non-finite values.
Results may differ from a plain program's by a relative error of at most 0.0075.
Values may be sent and summed in bfloat16 or wider, within the bound.
No kernel may reach another device: no remote copies, remote signals or barrier semaphores. Data moves between devices by JAX's collectives and lax.ppermute only.
A program may use at most 64 MiB of HBM per device.

v0:
```python
import math
import jax
import jax.numpy as jnp
from jax import lax
from jax.sharding import PartitionSpec as P

D = 1440
QH = 32
KVH = 4
HD = 64
TOP = 4
SLICES = 4
NEG_FILL = -1e30


def passed_along(value, axis, by):
    length = lax.axis_size(axis)
    return lax.ppermute(value, axis, [(i, (i + by) % length) for i in range(length)])


def attend_block(grouped, keys, values, query_pos, key_pos, state):
    run_max, run_sum, accum = state
    scores = jnp.einsum("rgjd,sgd->gjrs", grouped, keys, preferred_element_type=jnp.float32) * (
        1.0 / math.sqrt(HD)
    )
    allowed = key_pos[None, :] <= query_pos[:, None]
    scores = jnp.where(allowed[None, None], scores, NEG_FILL)
    new_max = jnp.maximum(run_max, jnp.max(scores, axis=-1))
    factor = jnp.exp(run_max - new_max)
    weights = jnp.exp(scores - new_max[..., None])
    run_sum = run_sum * factor + jnp.sum(weights, axis=-1)
    accum = accum * factor[..., None] + jnp.einsum(
        "gjrs,sgd->gjrd", weights, values.astype(jnp.float32), precision=lax.Precision.HIGHEST
    )
    return (new_max, run_sum, accum)


def body(
    query,
    key_value,
    positions,
    resid,
    sinks,
    o_weight,
    norm_gain,
    expert_ids,
    route_weights,
    w_gate,
    w_up,
    w_down,
):
    rows = query.shape[1]
    group = QH // KVH
    grouped = query[0].reshape(rows, KVH, group, HD)
    own_kv = key_value[0]
    own_pos = positions[0]
    start_max = jnp.broadcast_to(sinks.reshape(KVH, group)[:, :, None], (KVH, group, rows))
    state = (
        start_max,
        jnp.ones((KVH, group, rows), jnp.float32),
        jnp.zeros((KVH, group, rows, HD), jnp.float32),
    )

    def take(block, block_pos, carry):
        width = block.shape[0]
        keys = block[:, 0].reshape(width, KVH, HD)
        values = block[:, 1].reshape(width, KVH, HD)
        return attend_block(grouped, keys, values, own_pos, block_pos, carry)

    state = take(own_kv, own_pos, state)

    def turn(step, carry):
        block, block_pos, inner = carry
        block, block_pos = passed_along((block, block_pos), "ctx", 1)
        return (block, block_pos, take(block, block_pos, inner))

    state = lax.fori_loop(0, lax.axis_size("ctx") - 1, turn, (own_kv, own_pos, state))[2]
    run_max, run_sum, accum = state
    attended = accum / run_sum[..., None]
    attended = jnp.transpose(attended, (2, 0, 1, 3)).reshape(rows, QH * HD).astype(jnp.bfloat16)
    projected = jnp.dot(
        attended,
        lax.all_gather(o_weight, "exp", axis=0, tiled=True),
        preferred_element_type=jnp.float32,
    )
    mixed = resid[0].astype(jnp.float32) + projected
    normed = (
        mixed * lax.rsqrt(jnp.mean(mixed * mixed, axis=-1, keepdims=True) + 1e-05) * norm_gain
    ).astype(jnp.bfloat16)
    n_ctx = lax.axis_size("ctx")
    n_exp = lax.axis_size("exp")
    n_experts = n_ctx * n_exp // SLICES
    per_row = n_exp // SLICES
    cap = max(2, rows * TOP // n_experts)
    n_slots = n_experts * cap
    chosen = expert_ids[0].reshape(rows * TOP)
    onehot = (chosen[:, None] == jnp.arange(n_experts, dtype=jnp.int32)[None, :]).astype(jnp.int32)
    rank = jnp.sum((jnp.cumsum(onehot, axis=0) - onehot) * onehot, axis=1)
    slot = (chosen % per_row * n_ctx + chosen // per_row) * cap + rank
    source = (
        jnp.zeros((n_slots,), jnp.int32)
        .at[slot]
        .set(jnp.arange(rows * TOP, dtype=jnp.int32) // TOP)
    )
    filled = jnp.zeros((n_slots,), jnp.bool_).at[slot].set(True)
    outgoing = jnp.where(filled[:, None], normed[source], jnp.zeros((), jnp.bfloat16)).reshape(
        per_row, n_ctx, cap, D
    )
    arrived = lax.all_to_all(outgoing, "ctx", split_axis=1, concat_axis=1, tiled=True)
    copies = jnp.repeat(arrived, SLICES, axis=0)
    block = lax.all_to_all(copies, "exp", split_axis=0, concat_axis=0, tiled=True)
    flat = block.reshape(-1, D)
    gate = jnp.dot(flat, w_gate, preferred_element_type=jnp.float32)
    lifted = jnp.dot(flat, w_up, preferred_element_type=jnp.float32)
    active = (gate * jax.nn.sigmoid(1.702 * gate) * (lifted + 1.0)).astype(jnp.bfloat16)
    back = lax.all_to_all(
        jnp.dot(active, w_down, preferred_element_type=jnp.float32)
        .astype(jnp.bfloat16)
        .reshape(block.shape),
        "exp",
        split_axis=0,
        concat_axis=0,
        tiled=True,
    )
    count = back.shape[1]
    summed = jnp.sum(back.reshape(per_row, SLICES, count, cap, D).astype(jnp.float32), axis=1)
    result = summed.astype(jnp.bfloat16)
    returned = lax.all_to_all(result, "ctx", split_axis=1, concat_axis=1, tiled=True)
    picked = returned.reshape(n_slots, D)[slot].astype(jnp.float32).reshape(rows, TOP, D)
    final = mixed + jnp.sum(route_weights[0][:, :, None] * picked, axis=1)
    return final.astype(jnp.bfloat16)[None]


def solution(mesh):
    return jax.shard_map(
        body,
        mesh=mesh,
        in_specs=(
            P("exp", "ctx", None),
            P("exp", "ctx", None, None),
            P("exp", "ctx"),
            P("exp", "ctx", None),
            P(),
            P("exp", None),
            P(),
            P("exp", "ctx", None),
            P("exp", "ctx", None),
            P(None, ("ctx", "exp")),
            P(None, ("ctx", "exp")),
            P(("ctx", "exp"), None),
        ),
        out_specs=P("exp", "ctx", None),
        check_vma=False,
    )
```

profile of v0, /device:TPU:1, one launch (start us, length us, event | category | flops | bytes accessed | tf_op | source)
XLA Modules:
  0.0 688.6 jit_solution(17631098706521870149)
XLA Ops:
  17.1 230.6 %while.18 = (s32[]{:T(128)}, bf16[64,2,256]{2,0,1:T(8,128)(2,1)S(1)}, s32[64]{0:T(128)S(1)}, f32[4,8,64]{2,1,0:T(8,128)S(1)}, f32[4,8,64]{2,1,0:T(8,128)S(1)}, /...) while((s32[]{:T(128)}, ...), condition=%wide.region_5.6_spmd, body=%wide.region_2.5_spmd.sunk | while | flops 118759424 | bytes 3754157 | solution.py:77
  17.1 4.4 collective-permute-start.1
  21.5 3.5 collective-permute-start
  36.8 4.8 collective-permute-done.1
  41.6 4.9 collective-permute-done
  53.0 4.8 collective-permute-done.1
  67.7 4.4 collective-permute-done.1
  81.1 6.7 collective-permute-done.1
  87.9 21.1 %collective-permute-done = bf16[64,2,256]{2,0,1:T(8,128)(2,1)S(1)} collective-permute-done((bf16[64,2,256]{2,0,1:T(8,128)(2,1)S(1)}, bf16[64,2,256]{2,0,1:T(8,128)(2,1)S(1)}, u32[]{:S(2)}, u32[]{:S(2)}) %collective-permute-start) | collective-permute-done | bytes 65568 | tf_op jit(solution)/shard_map/while/body/eval_jaxpr/ppermute | solution.py:18
  115.4 4.8 collective-permute-done.1
  120.2 4.0 collective-permute-done
  130.7 4.4 collective-permute-done.1
  144.1 4.4 collective-permute-done.1
  157.5 4.4 collective-permute-done.1
  170.8 4.4 collective-permute-done.1
  184.2 4.7 collective-permute-done.1
  197.6 4.4 collective-permute-done.1
  211.0 4.4 collective-permute-done.1
  224.8 4.4 collective-permute-done.1
  238.2 4.4 collective-permute-done.1
  252.9 4.1 multiply_reduce_fusion.1
  260.2 16.6 %all_to_all.20 = bf16[8,16,2,1440]{3,2,0,1:T(2,128)(2,1)S(1)} all-to-all(bf16[8,16,2,1440]{3,2,0,1:T(2,128)(2,1)S(1)} %copy.69), channel_id=1, replica_groups=mesh['ctx'=16,'exp'=32] {'ctx'}, dimensions={1} | all-to-all | bytes 1474560 | tf_op jit(solution)/shard_map/all_to_all | solution.py:109
  280.1 183.5 %all_to_all.21 = bf16[32,16,2,1440]{3,2,1,0:T(2,128)(2,1)} all-to-all(bf16[32,16,2,1440]{3,2,1,0:T(2,128)(2,1)S(1)} %bitcast.67), channel_id=1, replica_groups=mesh['ctx'=16,'exp'=32] {'exp'}, dimensions={0} | all-to-all | bytes 5898240 | tf_op jit(solution)/shard_map/all_to_all | solution.py:111
  463.6 7.6 %reshape.250 = bf16[1024,1440]{1,0:T(8,128)(2,1)} reshape(bf16[32,16,2,1440]{3,2,1,0:T(2,128)(2,1)} %all_to_all.21) | data formatting | bytes 5898240 | tf_op jit(solution)/shard_map/reshape | solution.py:112
  471.2 4.4 fusion.37
  475.6 7.4 %convolution_convert_fusion = bf16[1024,1440]{0,1:T(8,128)(2,1)} fusion(bf16[360,1440]{1,0:T(8,128)(2,1)S(1)} %copy-done, f32[1024,360]{0,1:T(8,128)} %fusion.37, bf16[1024,1440]{1,0:T(8,128)(2,1)} %reshape.250, bf16[1440,360]{1,0:T(8,128)(2,1)} %param.24), kind=kOutput, calls=%fused_computation.19 | convolution fusion | flops 2127790080 | bytes 9446400 | tf_op jit(solution)/shard_map/dot_general | solution.py:117
  482.9 4.6 copy.71
  487.5 7.3 %reshape.251 = bf16[32,16,2,1440]{3,2,1,0:T(2,128)(2,1)} reshape(bf16[1024,1440]{1,0:T(8,128)(2,1)} %copy.71) | data formatting | bytes 5898240 | tf_op jit(solution)/shard_map/reshape | solution.py:119
  494.9 149.7 %all_to_all.22 = bf16[32,16,2,1440]{3,2,1,0:T(2,128)(2,1)S(1)} all-to-all(bf16[32,16,2,1440]{3,2,1,0:T(2,128)(2,1)} %reshape.251), channel_id=1, replica_groups=mesh['ctx'=16,'exp'=32] {'exp'}, dimensions={0} | all-to-all | bytes 5898240 | tf_op jit(solution)/shard_map/all_to_all | solution.py:116
  644.5 3.5 bitcast_reduce_fusion
  649.7 3.9 all-to-all-start.3
  653.7 21.3 %all-to-all-done.3 = bf16[8,16,2,1440]{3,2,0,1:T(2,128)(2,1)S(1)} async-done(((bf16[8,16,2,1440]{3,2,0,1:T(2,128)(2,1)}), bf16[8,16,2,1440]{3,2,0,1:T(2,128)(2,1)S(1)}, u32[]{:S(2)}, u32[]{:S(2)}) %all-to-all-start.3) | async-done | bytes 737312 | tf_op jit(solution)/shard_map/all_to_all | solution.py:128
  (295 shorter events, 156.7 us)
Async XLA Ops:
  6.5 246.3 %all-gather.2.cloned.1.call-start = ((), (), s32[]{:S(2)}) async-start(), calls=%async_computation.4 | async-start | bytes 6488064 | tf_op jit(solution)/shard_map/all_gather | solution.py:83
  17.1 10.5 %collective-permute-start.1 = (s32[64]{0:T(128)S(1)}, s32[64]{0:T(128)S(1)}, u32[]{:S(2)}, u32[]{:S(2)}) collective-permute-start(s32[64]{0:T(128)S(1)} %get-tuple-element.176), channel_id=1, source_target_pairs={{0,32},{32,64},{64,96},{96,128},{128,160},{160,192},{192,224},{224... | collective-permute-start | bytes 776 | tf_op jit(solution)/shard_map/while/body/eval_jaxpr/ppermute | solution.py:18
  21.5 8.9 %collective-permute-start = (bf16[64,2,256]{2,0,1:T(8,128)(2,1)S(1)}, bf16[64,2,256]{2,0,1:T(8,128)(2,1)S(1)}, u32[]{:S(2)}, u32[]{:S(2)}) collective-permute-start(bf16[64,2,256]{2,0,1:T(8,128)(2,1)S(1)} %get-tuple-element.175), channel_id=1, source_target_pairs={{0,32},{32,64},{64,96},{96,128},{128,160},{160,192},{192,224},{224... | collective-permute-start | bytes 196616 | tf_op jit(solution)/shard_map/while/body/eval_jaxpr/ppermute | solution.py:18
  32.9 8.6 %collective-permute-start.1 = (s32[64]{0:T(128)S(1)}, s32[64]{0:T(128)S(1)}, u32[]{:S(2)}, u32[]{:S(2)}) collective-permute-start(s32[64]{0:T(128)S(1)} %get-tuple-element.176), channel_id=1, source_target_pairs={{0,32},{32,64},{64,96},{96,128},{128,160},{160,192},{192,224},{224... | collective-permute-start | bytes 776 | tf_op jit(solution)/shard_map/while/body/eval_jaxpr/ppermute | solution.py:18
  34.8 11.7 %collective-permute-start = (bf16[64,2,256]{2,0,1:T(8,128)(2,1)S(1)}, bf16[64,2,256]{2,0,1:T(8,128)(2,1)S(1)}, u32[]{:S(2)}, u32[]{:S(2)}) collective-permute-start(bf16[64,2,256]{2,0,1:T(8,128)(2,1)S(1)} %get-tuple-element.175), channel_id=1, source_target_pairs={{0,32},{32,64},{64,96},{96,128},{128,160},{160,192},{192,224},{224... | collective-permute-start | bytes 196616 | tf_op jit(solution)/shard_map/while/body/eval_jaxpr/ppermute | solution.py:18
  49.1 8.6 %collective-permute-start.1 = (s32[64]{0:T(128)S(1)}, s32[64]{0:T(128)S(1)}, u32[]{:S(2)}, u32[]{:S(2)}) collective-permute-start(s32[64]{0:T(128)S(1)} %get-tuple-element.176), channel_id=1, source_target_pairs={{0,32},{32,64},{64,96},{96,128},{128,160},{160,192},{192,224},{224... | collective-permute-start | bytes 776 | tf_op jit(solution)/shard_map/while/body/eval_jaxpr/ppermute | solution.py:18
  51.0 10.3 %collective-permute-start = (bf16[64,2,256]{2,0,1:T(8,128)(2,1)S(1)}, bf16[64,2,256]{2,0,1:T(8,128)(2,1)S(1)}, u32[]{:S(2)}, u32[]{:S(2)}) collective-permute-start(bf16[64,2,256]{2,0,1:T(8,128)(2,1)S(1)} %get-tuple-element.175), channel_id=1, source_target_pairs={{0,32},{32,64},{64,96},{96,128},{128,160},{160,192},{192,224},{224... | collective-permute-start | bytes 196616 | tf_op jit(solution)/shard_map/while/body/eval_jaxpr/ppermute | solution.py:18
  63.8 8.2 %collective-permute-start.1 = (s32[64]{0:T(128)S(1)}, s32[64]{0:T(128)S(1)}, u32[]{:S(2)}, u32[]{:S(2)}) collective-permute-start(s32[64]{0:T(128)S(1)} %get-tuple-element.176), channel_id=1, source_target_pairs={{0,32},{32,64},{64,96},{96,128},{128,160},{160,192},{192,224},{224... | collective-permute-start | bytes 776 | tf_op jit(solution)/shard_map/while/body/eval_jaxpr/ppermute | solution.py:18
  65.8 8.9 %collective-permute-start = (bf16[64,2,256]{2,0,1:T(8,128)(2,1)S(1)}, bf16[64,2,256]{2,0,1:T(8,128)(2,1)S(1)}, u32[]{:S(2)}, u32[]{:S(2)}) collective-permute-start(bf16[64,2,256]{2,0,1:T(8,128)(2,1)S(1)} %get-tuple-element.175), channel_id=1, source_target_pairs={{0,32},{32,64},{64,96},{96,128},{128,160},{160,192},{192,224},{224... | collective-permute-start | bytes 196616 | tf_op jit(solution)/shard_map/while/body/eval_jaxpr/ppermute | solution.py:18
  77.2 10.6 %collective-permute-start.1 = (s32[64]{0:T(128)S(1)}, s32[64]{0:T(128)S(1)}, u32[]{:S(2)}, u32[]{:S(2)}) collective-permute-start(s32[64]{0:T(128)S(1)} %get-tuple-element.176), channel_id=1, source_target_pairs={{0,32},{32,64},{64,96},{96,128},{128,160},{160,192},{192,224},{224... | collective-permute-start | bytes 776 | tf_op jit(solution)/shard_map/while/body/eval_jaxpr/ppermute | solution.py:18
  79.2 29.8 %collective-permute-start = (bf16[64,2,256]{2,0,1:T(8,128)(2,1)S(1)}, bf16[64,2,256]{2,0,1:T(8,128)(2,1)S(1)}, u32[]{:S(2)}, u32[]{:S(2)}) collective-permute-start(bf16[64,2,256]{2,0,1:T(8,128)(2,1)S(1)} %get-tuple-element.175), channel_id=1, source_target_pairs={{0,32},{32,64},{64,96},{96,128},{128,160},{160,192},{192,224},{224... | collective-permute-start | bytes 196616 | tf_op jit(solution)/shard_map/while/body/eval_jaxpr/ppermute | solution.py:18
  111.5 8.6 %collective-permute-start.1 = (s32[64]{0:T(128)S(1)}, s32[64]{0:T(128)S(1)}, u32[]{:S(2)}, u32[]{:S(2)}) collective-permute-start(s32[64]{0:T(128)S(1)} %get-tuple-element.176), channel_id=1, source_target_pairs={{0,32},{32,64},{64,96},{96,128},{128,160},{160,192},{192,224},{224... | collective-permute-start | bytes 776 | tf_op jit(solution)/shard_map/while/body/eval_jaxpr/ppermute | solution.py:18
  113.5 10.8 %collective-permute-start = (bf16[64,2,256]{2,0,1:T(8,128)(2,1)S(1)}, bf16[64,2,256]{2,0,1:T(8,128)(2,1)S(1)}, u32[]{:S(2)}, u32[]{:S(2)}) collective-permute-start(bf16[64,2,256]{2,0,1:T(8,128)(2,1)S(1)} %get-tuple-element.175), channel_id=1, source_target_pairs={{0,32},{32,64},{64,96},{96,128},{128,160},{160,192},{192,224},{224... | collective-permute-start | bytes 196616 | tf_op jit(solution)/shard_map/while/body/eval_jaxpr/ppermute | solution.py:18
  126.8 8.2 %collective-permute-start.1 = (s32[64]{0:T(128)S(1)}, s32[64]{0:T(128)S(1)}, u32[]{:S(2)}, u32[]{:S(2)}) collective-permute-start(s32[64]{0:T(128)S(1)} %get-tuple-element.176), channel_id=1, source_target_pairs={{0,32},{32,64},{64,96},{96,128},{128,160},{160,192},{192,224},{224... | collective-permute-start | bytes 776 | tf_op jit(solution)/shard_map/while/body/eval_jaxpr/ppermute | solution.py:18
  128.7 8.9 %collective-permute-start = (bf16[64,2,256]{2,0,1:T(8,128)(2,1)S(1)}, bf16[64,2,256]{2,0,1:T(8,128)(2,1)S(1)}, u32[]{:S(2)}, u32[]{:S(2)}) collective-permute-start(bf16[64,2,256]{2,0,1:T(8,128)(2,1)S(1)} %get-tuple-element.175), channel_id=1, source_target_pairs={{0,32},{32,64},{64,96},{96,128},{128,160},{160,192},{192,224},{224... | collective-permute-start | bytes 196616 | tf_op jit(solution)/shard_map/while/body/eval_jaxpr/ppermute | solution.py:18
  140.2 8.2 %collective-permute-start.1 = (s32[64]{0:T(128)S(1)}, s32[64]{0:T(128)S(1)}, u32[]{:S(2)}, u32[]{:S(2)}) collective-permute-start(s32[64]{0:T(128)S(1)} %get-tuple-element.176), channel_id=1, source_target_pairs={{0,32},{32,64},{64,96},{96,128},{128,160},{160,192},{192,224},{224... | collective-permute-start | bytes 776 | tf_op jit(solution)/shard_map/while/body/eval_jaxpr/ppermute | solution.py:18
  142.1 8.9 %collective-permute-start = (bf16[64,2,256]{2,0,1:T(8,128)(2,1)S(1)}, bf16[64,2,256]{2,0,1:T(8,128)(2,1)S(1)}, u32[]{:S(2)}, u32[]{:S(2)}) collective-permute-start(bf16[64,2,256]{2,0,1:T(8,128)(2,1)S(1)} %get-tuple-element.175), channel_id=1, source_target_pairs={{0,32},{32,64},{64,96},{96,128},{128,160},{160,192},{192,224},{224... | collective-permute-start | bytes 196616 | tf_op jit(solution)/shard_map/while/body/eval_jaxpr/ppermute | solution.py:18
  153.6 8.2 %collective-permute-start.1 = (s32[64]{0:T(128)S(1)}, s32[64]{0:T(128)S(1)}, u32[]{:S(2)}, u32[]{:S(2)}) collective-permute-start(s32[64]{0:T(128)S(1)} %get-tuple-element.176), channel_id=1, source_target_pairs={{0,32},{32,64},{64,96},{96,128},{128,160},{160,192},{192,224},{224... | collective-permute-start | bytes 776 | tf_op jit(solution)/shard_map/while/body/eval_jaxpr/ppermute | solution.py:18
  155.5 8.9 %collective-permute-start = (bf16[64,2,256]{2,0,1:T(8,128)(2,1)S(1)}, bf16[64,2,256]{2,0,1:T(8,128)(2,1)S(1)}, u32[]{:S(2)}, u32[]{:S(2)}) collective-permute-start(bf16[64,2,256]{2,0,1:T(8,128)(2,1)S(1)} %get-tuple-element.175), channel_id=1, source_target_pairs={{0,32},{32,64},{64,96},{96,128},{128,160},{160,192},{192,224},{224... | collective-permute-start | bytes 196616 | tf_op jit(solution)/shard_map/while/body/eval_jaxpr/ppermute | solution.py:18
  167.0 8.2 %collective-permute-start.1 = (s32[64]{0:T(128)S(1)}, s32[64]{0:T(128)S(1)}, u32[]{:S(2)}, u32[]{:S(2)}) collective-permute-start(s32[64]{0:T(128)S(1)} %get-tuple-element.176), channel_id=1, source_target_pairs={{0,32},{32,64},{64,96},{96,128},{128,160},{160,192},{192,224},{224... | collective-permute-start | bytes 776 | tf_op jit(solution)/shard_map/while/body/eval_jaxpr/ppermute | solution.py:18
  168.9 8.9 %collective-permute-start = (bf16[64,2,256]{2,0,1:T(8,128)(2,1)S(1)}, bf16[64,2,256]{2,0,1:T(8,128)(2,1)S(1)}, u32[]{:S(2)}, u32[]{:S(2)}) collective-permute-start(bf16[64,2,256]{2,0,1:T(8,128)(2,1)S(1)} %get-tuple-element.175), channel_id=1, source_target_pairs={{0,32},{32,64},{64,96},{96,128},{128,160},{160,192},{192,224},{224... | collective-permute-start | bytes 196616 | tf_op jit(solution)/shard_map/while/body/eval_jaxpr/ppermute | solution.py:18
  180.4 8.5 %collective-permute-start.1 = (s32[64]{0:T(128)S(1)}, s32[64]{0:T(128)S(1)}, u32[]{:S(2)}, u32[]{:S(2)}) collective-permute-start(s32[64]{0:T(128)S(1)} %get-tuple-element.176), channel_id=1, source_target_pairs={{0,32},{32,64},{64,96},{96,128},{128,160},{160,192},{192,224},{224... | collective-permute-start | bytes 776 | tf_op jit(solution)/shard_map/while/body/eval_jaxpr/ppermute | solution.py:18
  182.3 8.9 %collective-permute-start = (bf16[64,2,256]{2,0,1:T(8,128)(2,1)S(1)}, bf16[64,2,256]{2,0,1:T(8,128)(2,1)S(1)}, u32[]{:S(2)}, u32[]{:S(2)}) collective-permute-start(bf16[64,2,256]{2,0,1:T(8,128)(2,1)S(1)} %get-tuple-element.175), channel_id=1, source_target_pairs={{0,32},{32,64},{64,96},{96,128},{128,160},{160,192},{192,224},{224... | collective-permute-start | bytes 196616 | tf_op jit(solution)/shard_map/while/body/eval_jaxpr/ppermute | solution.py:18
  193.8 8.2 %collective-permute-start.1 = (s32[64]{0:T(128)S(1)}, s32[64]{0:T(128)S(1)}, u32[]{:S(2)}, u32[]{:S(2)}) collective-permute-start(s32[64]{0:T(128)S(1)} %get-tuple-element.176), channel_id=1, source_target_pairs={{0,32},{32,64},{64,96},{96,128},{128,160},{160,192},{192,224},{224... | collective-permute-start | bytes 776 | tf_op jit(solution)/shard_map/while/body/eval_jaxpr/ppermute | solution.py:18
  195.7 8.9 %collective-permute-start = (bf16[64,2,256]{2,0,1:T(8,128)(2,1)S(1)}, bf16[64,2,256]{2,0,1:T(8,128)(2,1)S(1)}, u32[]{:S(2)}, u32[]{:S(2)}) collective-permute-start(bf16[64,2,256]{2,0,1:T(8,128)(2,1)S(1)} %get-tuple-element.175), channel_id=1, source_target_pairs={{0,32},{32,64},{64,96},{96,128},{128,160},{160,192},{192,224},{224... | collective-permute-start | bytes 196616 | tf_op jit(solution)/shard_map/while/body/eval_jaxpr/ppermute | solution.py:18
  207.2 8.2 %collective-permute-start.1 = (s32[64]{0:T(128)S(1)}, s32[64]{0:T(128)S(1)}, u32[]{:S(2)}, u32[]{:S(2)}) collective-permute-start(s32[64]{0:T(128)S(1)} %get-tuple-element.176), channel_id=1, source_target_pairs={{0,32},{32,64},{64,96},{96,128},{128,160},{160,192},{192,224},{224... | collective-permute-start | bytes 776 | tf_op jit(solution)/shard_map/while/body/eval_jaxpr/ppermute | solution.py:18
  209.1 9.3 %collective-permute-start = (bf16[64,2,256]{2,0,1:T(8,128)(2,1)S(1)}, bf16[64,2,256]{2,0,1:T(8,128)(2,1)S(1)}, u32[]{:S(2)}, u32[]{:S(2)}) collective-permute-start(bf16[64,2,256]{2,0,1:T(8,128)(2,1)S(1)} %get-tuple-element.175), channel_id=1, source_target_pairs={{0,32},{32,64},{64,96},{96,128},{128,160},{160,192},{192,224},{224... | collective-permute-start | bytes 196616 | tf_op jit(solution)/shard_map/while/body/eval_jaxpr/ppermute | solution.py:18
  220.9 8.2 %collective-permute-start.1 = (s32[64]{0:T(128)S(1)}, s32[64]{0:T(128)S(1)}, u32[]{:S(2)}, u32[]{:S(2)}) collective-permute-start(s32[64]{0:T(128)S(1)} %get-tuple-element.176), channel_id=1, source_target_pairs={{0,32},{32,64},{64,96},{96,128},{128,160},{160,192},{192,224},{224... | collective-permute-start | bytes 776 | tf_op jit(solution)/shard_map/while/body/eval_jaxpr/ppermute | solution.py:18
  222.9 8.9 %collective-permute-start = (bf16[64,2,256]{2,0,1:T(8,128)(2,1)S(1)}, bf16[64,2,256]{2,0,1:T(8,128)(2,1)S(1)}, u32[]{:S(2)}, u32[]{:S(2)}) collective-permute-start(bf16[64,2,256]{2,0,1:T(8,128)(2,1)S(1)} %get-tuple-element.175), channel_id=1, source_target_pairs={{0,32},{32,64},{64,96},{96,128},{128,160},{160,192},{192,224},{224... | collective-permute-start | bytes 196616 | tf_op jit(solution)/shard_map/while/body/eval_jaxpr/ppermute | solution.py:18
  234.3 8.2 %collective-permute-start.1 = (s32[64]{0:T(128)S(1)}, s32[64]{0:T(128)S(1)}, u32[]{:S(2)}, u32[]{:S(2)}) collective-permute-start(s32[64]{0:T(128)S(1)} %get-tuple-element.176), channel_id=1, source_target_pairs={{0,32},{32,64},{64,96},{96,128},{128,160},{160,192},{192,224},{224... | collective-permute-start | bytes 776 | tf_op jit(solution)/shard_map/while/body/eval_jaxpr/ppermute | solution.py:18
  236.3 8.9 %collective-permute-start = (bf16[64,2,256]{2,0,1:T(8,128)(2,1)S(1)}, bf16[64,2,256]{2,0,1:T(8,128)(2,1)S(1)}, u32[]{:S(2)}, u32[]{:S(2)}) collective-permute-start(bf16[64,2,256]{2,0,1:T(8,128)(2,1)S(1)} %get-tuple-element.175), channel_id=1, source_target_pairs={{0,32},{32,64},{64,96},{96,128},{128,160},{160,192},{192,224},{224... | collective-permute-start | bytes 196616 | tf_op jit(solution)/shard_map/while/body/eval_jaxpr/ppermute | solution.py:18
  649.7 25.3 %all-to-all-start.3 = ((bf16[8,16,2,1440]{3,2,0,1:T(2,128)(2,1)}), bf16[8,16,2,1440]{3,2,0,1:T(2,128)(2,1)S(1)}, u32[]{:S(2)}, u32[]{:S(2)}) async-start(bf16[8,16,2,1440]{3,2,0,1:T(2,128)(2,1)} %copy.72), calls=%async_computation.3 | async-start | bytes 1572864 | tf_op jit(solution)/shard_map/all_to_all | solution.py:128
  (8 other events, 500.7 us)
Sparse Core Ops, SparseCore 0:
  10.5 115.4 all-gather.1
where the time goes:
time: 690 us; the launch traced here: 689 us
  blocking collectives  350 us (51%)
  waiting for transfers between devices  151 us (22%)
  starting transfers between devices  65.6 us (10%)
  matrix products  48.6 us (7%)
  local copies, waits for them, and re-layouts  44.8 us (6%)
  between operations  13.7 us (2%)
  other arithmetic  13.4 us (2%)
    all_to_all x1, blocking collectives, body(): lax.all_to_all(copies, 'exp', split_axis=0, concat_axis=0, tiled=True)  183 us
    all_to_all x1, blocking collectives, body(): lax.all_to_all(jnp.dot(active, w_down, preferred_element_type=jnp.float32...  150 us
    ppermute x30, waiting for transfers between devices, passed_along(): lax.ppermute(value, axis, [(i, (i + by) % length) for i in range(length)])  129 us
    ppermute x30, starting transfers between devices, passed_along(): lax.ppermute(value, axis, [(i, (i + by) % length) for i in range(length)])  61.7 us
    dot_general x16, matrix products, attend_block(): jnp.einsum('gjrs,sgd->gjrd', weights, values.astype(jnp.float32), precisi...  22.6 us
    all_to_all x1, waiting for transfers between devices, body(): lax.all_to_all(result, 'ctx', split_axis=1, concat_axis=1, tiled=True)  21.3 us
    all_to_all x1, blocking collectives, body(): lax.all_to_all(outgoing, 'ctx', split_axis=1, concat_axis=1, tiled=True)  16.6 us
  transfers between devices with their start and end apart: 32, of which 31 were waited for; matrix products, arithmetic and copies ran while one was open for 8% of the time, Pallas kernels for 0%

commit v1 on v0

--- a/solution.py
+++ b/solution.py
@@ -49,6 +49,13 @@
     w_up,
     w_down,
 ):
+
+    def expand_islands_all(z, axis_k, along_dim):
+        return jnp.concatenate(
+            lax.all_to_all(jnp.stack(jnp.split(z, lax.axis_size("ctx"), axis_k), 0), "ctx", 0, 0),
+            along_dim,
+        )
+
     rows = query.shape[1]
     group = QH // KVH
     grouped = query[0].reshape(rows, KVH, group, HD)
@@ -125,7 +132,7 @@
     count = back.shape[1]
     summed = jnp.sum(back.reshape(per_row, SLICES, count, cap, D).astype(jnp.float32), axis=1)
     result = summed.astype(jnp.bfloat16)
-    returned = lax.all_to_all(result, "ctx", split_axis=1, concat_axis=1, tiled=True)
+    returned = expand_islands_all(result, 1, along_dim=1)
     picked = returned.reshape(n_slots, D)[slot].astype(jnp.float32).reshape(rows, TOP, D)
     final = mixed + jnp.sum(route_weights[0][:, :, None] * picked, axis=1)
     return final.astype(jnp.bfloat16)[None]

time: 690 us -> 699 us (1.013)
  local copies, waits for them, and re-layouts: 44.8 us -> 53.5 us
    unnamed x20 -> x35, local copies, waits for them, and re-layouts: 3.25 us -> 13 us
  transfers between devices with their start and end apart: 32 -> 32, of which waited for: 31 -> 31; matrix products, arithmetic and copies ran while one was open for 8% -> 7% of each run, Pallas kernels for 0% -> 0%
where the time goes in v1:
time: 699 us; the launch traced here: 698 us
  blocking collectives  350 us (50%)
  waiting for transfers between devices  151 us (22%)
  starting transfers between devices  65.8 us (9%)
  local copies, waits for them, and re-layouts  53.5 us (8%)
  matrix products  48.6 us (7%)
  between operations  13.7 us (2%)
  other arithmetic  13.4 us (2%)
    all_to_all x1, blocking collectives, body(): lax.all_to_all(copies, 'exp', split_axis=0, concat_axis=0, tiled=True)  183 us
    all_to_all x1, blocking collectives, body(): lax.all_to_all(jnp.dot(active, w_down, preferred_element_type=jnp.float32...  150 us
    ppermute x30, waiting for transfers between devices, passed_along(): lax.ppermute(value, axis, [(i, (i + by) % length) for i in range(length)])  129 us
    ppermute x30, starting transfers between devices, passed_along(): lax.ppermute(value, axis, [(i, (i + by) % length) for i in range(length)])  61.7 us
    dot_general x16, matrix products, attend_block(): jnp.einsum('gjrs,sgd->gjrd', weights, values.astype(jnp.float32), precisi...  22.6 us
    all_to_all x1, waiting for transfers between devices, expand_islands_all(): lax.all_to_all(jnp.stack(jnp.split(z, lax.axis_size('ctx'), axis_k), 0),...  21.3 us
    all_to_all x1, blocking collectives, body(): lax.all_to_all(outgoing, 'ctx', split_axis=1, concat_axis=1, tiled=True)  16.6 us
  transfers between devices with their start and end apart: 32, of which 31 were waited for; matrix products, arithmetic and copies ran while one was open for 7% of the time, Pallas kernels for 0%

profile of v1, /device:TPU:1, one launch (start us, length us, event | category | flops | bytes accessed | tf_op | source)
XLA Modules:
  0.0 697.6 jit_solution(8061797299389640998)
XLA Ops:
  17.1 230.6 %while.18 = (s32[]{:T(128)}, bf16[64,2,256]{2,0,1:T(8,128)(2,1)S(1)}, s32[64]{0:T(128)S(1)}, f32[4,8,64]{2,1,0:T(8,128)S(1)}, f32[4,8,64]{2,1,0:T(8,128)S(1)}, /...) while((s32[]{:T(128)}, ...), condition=%wide.region_5.6_spmd, body=%wide.region_2.5_spmd.sunk | while | flops 118759424 | bytes 3754157 | solution.py:84
  17.1 4.4 collective-permute-start.1
  21.5 3.5 collective-permute-start
  36.8 4.8 collective-permute-done.1
  41.6 4.9 collective-permute-done
  53.0 4.8 collective-permute-done.1
  67.7 4.4 collective-permute-done.1
  81.1 6.7 collective-permute-done.1
  87.9 21.1 %collective-permute-done = bf16[64,2,256]{2,0,1:T(8,128)(2,1)S(1)} collective-permute-done((bf16[64,2,256]{2,0,1:T(8,128)(2,1)S(1)}, bf16[64,2,256]{2,0,1:T(8,128)(2,1)S(1)}, u32[]{:S(2)}, u32[]{:S(2)}) %collective-permute-start) | collective-permute-done | bytes 65568 | tf_op jit(solution)/shard_map/while/body/eval_jaxpr/ppermute | solution.py:18
  115.4 4.8 collective-permute-done.1
  120.2 4.0 collective-permute-done
  130.7 4.4 collective-permute-done.1
  144.1 4.4 collective-permute-done.1
  157.5 4.4 collective-permute-done.1
  170.8 4.4 collective-permute-done.1
  184.2 4.7 collective-permute-done.1
  197.6 4.4 collective-permute-done.1
  211.0 4.4 collective-permute-done.1
  224.8 4.4 collective-permute-done.1
  238.2 4.4 collective-permute-done.1
  252.9 4.1 multiply_reduce_fusion.1
  260.2 16.6 %all_to_all.20 = bf16[8,16,2,1440]{3,2,0,1:T(2,128)(2,1)S(1)} all-to-all(bf16[8,16,2,1440]{3,2,0,1:T(2,128)(2,1)S(1)} %copy.79), channel_id=1, replica_groups=mesh['ctx'=16,'exp'=32] {'ctx'}, dimensions={1} | all-to-all | bytes 1474560 | tf_op jit(solution)/shard_map/all_to_all | solution.py:116
  280.1 183.5 %all_to_all.21 = bf16[32,16,2,1440]{3,2,1,0:T(2,128)(2,1)} all-to-all(bf16[32,16,2,1440]{3,2,1,0:T(2,128)(2,1)S(1)} %bitcast.164), channel_id=1, replica_groups=mesh['ctx'=16,'exp'=32] {'exp'}, dimensions={0} | all-to-all | bytes 5898240 | tf_op jit(solution)/shard_map/all_to_all | solution.py:118
  463.6 7.6 %reshape.250 = bf16[1024,1440]{1,0:T(8,128)(2,1)} reshape(bf16[32,16,2,1440]{3,2,1,0:T(2,128)(2,1)} %all_to_all.21) | data formatting | bytes 5898240 | tf_op jit(solution)/shard_map/reshape | solution.py:119
  471.2 4.4 fusion.53
  475.6 7.4 %convolution_convert_fusion = bf16[1024,1440]{0,1:T(8,128)(2,1)} fusion(bf16[360,1440]{1,0:T(8,128)(2,1)S(1)} %copy-done, f32[1024,360]{0,1:T(8,128)} %fusion.53, bf16[1024,1440]{1,0:T(8,128)(2,1)} %reshape.250, bf16[1440,360]{1,0:T(8,128)(2,1)} %param.24), kind=kOutput, calls=%fused_computation.19 | convolution fusion | flops 2127790080 | bytes 9446400 | tf_op jit(solution)/shard_map/dot_general | solution.py:124
  482.9 4.6 copy.81
  487.5 7.3 %reshape.251 = bf16[32,16,2,1440]{3,2,1,0:T(2,128)(2,1)} reshape(bf16[1024,1440]{1,0:T(8,128)(2,1)} %copy.81) | data formatting | bytes 5898240 | tf_op jit(solution)/shard_map/reshape | solution.py:126
  494.9 149.7 %all_to_all.22 = bf16[32,16,2,1440]{3,2,1,0:T(2,128)(2,1)S(1)} all-to-all(bf16[32,16,2,1440]{3,2,1,0:T(2,128)(2,1)} %reshape.251), channel_id=1, replica_groups=mesh['ctx'=16,'exp'=32] {'exp'}, dimensions={0} | all-to-all | bytes 5898240 | tf_op jit(solution)/shard_map/all_to_all | solution.py:123
  644.5 3.5 bitcast_reduce_fusion
  658.4 4.1 all-to-all-start.3
  662.7 21.3 %all-to-all-done.3 = bf16[16,8,1,2,1440]{4,3,1,2,0:T(2,128)(2,1)S(1)} async-done(((bf16[16,8,1,2,1440]{4,3,1,2,0:T(2,128)(2,1)}), bf16[16,8,1,2,1440]{4,3,1,2,0:T(2,128)(2,1)S(1)}, u32[]{:S(2)}, u32[]{:S(2)}) %all-to-all-start.3) | async-done | bytes 737312 | tf_op jit(solution)/shard_map/all_to_all | solution.py:55
  (309 shorter events, 165.4 us)
Async XLA Ops:
  6.5 246.3 %all-gather.2.cloned.1.call-start = ((), (), s32[]{:S(2)}) async-start(), calls=%async_computation.4 | async-start | bytes 6488064 | tf_op jit(solution)/shard_map/all_gather | solution.py:90
  17.1 10.5 %collective-permute-start.1 = (s32[64]{0:T(128)S(1)}, s32[64]{0:T(128)S(1)}, u32[]{:S(2)}, u32[]{:S(2)}) collective-permute-start(s32[64]{0:T(128)S(1)} %get-tuple-element.170), channel_id=1, source_target_pairs={{0,32},{32,64},{64,96},{96,128},{128,160},{160,192},{192,224},{224... | collective-permute-start | bytes 776 | tf_op jit(solution)/shard_map/while/body/eval_jaxpr/ppermute | solution.py:18
  21.5 8.9 %collective-permute-start = (bf16[64,2,256]{2,0,1:T(8,128)(2,1)S(1)}, bf16[64,2,256]{2,0,1:T(8,128)(2,1)S(1)}, u32[]{:S(2)}, u32[]{:S(2)}) collective-permute-start(bf16[64,2,256]{2,0,1:T(8,128)(2,1)S(1)} %get-tuple-element.169), channel_id=1, source_target_pairs={{0,32},{32,64},{64,96},{96,128},{128,160},{160,192},{192,224},{224... | collective-permute-start | bytes 196616 | tf_op jit(solution)/shard_map/while/body/eval_jaxpr/ppermute | solution.py:18
  32.9 8.6 %collective-permute-start.1 = (s32[64]{0:T(128)S(1)}, s32[64]{0:T(128)S(1)}, u32[]{:S(2)}, u32[]{:S(2)}) collective-permute-start(s32[64]{0:T(128)S(1)} %get-tuple-element.170), channel_id=1, source_target_pairs={{0,32},{32,64},{64,96},{96,128},{128,160},{160,192},{192,224},{224... | collective-permute-start | bytes 776 | tf_op jit(solution)/shard_map/while/body/eval_jaxpr/ppermute | solution.py:18
  34.8 11.7 %collective-permute-start = (bf16[64,2,256]{2,0,1:T(8,128)(2,1)S(1)}, bf16[64,2,256]{2,0,1:T(8,128)(2,1)S(1)}, u32[]{:S(2)}, u32[]{:S(2)}) collective-permute-start(bf16[64,2,256]{2,0,1:T(8,128)(2,1)S(1)} %get-tuple-element.169), channel_id=1, source_target_pairs={{0,32},{32,64},{64,96},{96,128},{128,160},{160,192},{192,224},{224... | collective-permute-start | bytes 196616 | tf_op jit(solution)/shard_map/while/body/eval_jaxpr/ppermute | solution.py:18
  49.1 8.6 %collective-permute-start.1 = (s32[64]{0:T(128)S(1)}, s32[64]{0:T(128)S(1)}, u32[]{:S(2)}, u32[]{:S(2)}) collective-permute-start(s32[64]{0:T(128)S(1)} %get-tuple-element.170), channel_id=1, source_target_pairs={{0,32},{32,64},{64,96},{96,128},{128,160},{160,192},{192,224},{224... | collective-permute-start | bytes 776 | tf_op jit(solution)/shard_map/while/body/eval_jaxpr/ppermute | solution.py:18
  51.0 10.3 %collective-permute-start = (bf16[64,2,256]{2,0,1:T(8,128)(2,1)S(1)}, bf16[64,2,256]{2,0,1:T(8,128)(2,1)S(1)}, u32[]{:S(2)}, u32[]{:S(2)}) collective-permute-start(bf16[64,2,256]{2,0,1:T(8,128)(2,1)S(1)} %get-tuple-element.169), channel_id=1, source_target_pairs={{0,32},{32,64},{64,96},{96,128},{128,160},{160,192},{192,224},{224... | collective-permute-start | bytes 196616 | tf_op jit(solution)/shard_map/while/body/eval_jaxpr/ppermute | solution.py:18
  63.8 8.2 %collective-permute-start.1 = (s32[64]{0:T(128)S(1)}, s32[64]{0:T(128)S(1)}, u32[]{:S(2)}, u32[]{:S(2)}) collective-permute-start(s32[64]{0:T(128)S(1)} %get-tuple-element.170), channel_id=1, source_target_pairs={{0,32},{32,64},{64,96},{96,128},{128,160},{160,192},{192,224},{224... | collective-permute-start | bytes 776 | tf_op jit(solution)/shard_map/while/body/eval_jaxpr/ppermute | solution.py:18
  65.8 8.9 %collective-permute-start = (bf16[64,2,256]{2,0,1:T(8,128)(2,1)S(1)}, bf16[64,2,256]{2,0,1:T(8,128)(2,1)S(1)}, u32[]{:S(2)}, u32[]{:S(2)}) collective-permute-start(bf16[64,2,256]{2,0,1:T(8,128)(2,1)S(1)} %get-tuple-element.169), channel_id=1, source_target_pairs={{0,32},{32,64},{64,96},{96,128},{128,160},{160,192},{192,224},{224... | collective-permute-start | bytes 196616 | tf_op jit(solution)/shard_map/while/body/eval_jaxpr/ppermute | solution.py:18
  77.2 10.6 %collective-permute-start.1 = (s32[64]{0:T(128)S(1)}, s32[64]{0:T(128)S(1)}, u32[]{:S(2)}, u32[]{:S(2)}) collective-permute-start(s32[64]{0:T(128)S(1)} %get-tuple-element.170), channel_id=1, source_target_pairs={{0,32},{32,64},{64,96},{96,128},{128,160},{160,192},{192,224},{224... | collective-permute-start | bytes 776 | tf_op jit(solution)/shard_map/while/body/eval_jaxpr/ppermute | solution.py:18
  79.2 29.8 %collective-permute-start = (bf16[64,2,256]{2,0,1:T(8,128)(2,1)S(1)}, bf16[64,2,256]{2,0,1:T(8,128)(2,1)S(1)}, u32[]{:S(2)}, u32[]{:S(2)}) collective-permute-start(bf16[64,2,256]{2,0,1:T(8,128)(2,1)S(1)} %get-tuple-element.169), channel_id=1, source_target_pairs={{0,32},{32,64},{64,96},{96,128},{128,160},{160,192},{192,224},{224... | collective-permute-start | bytes 196616 | tf_op jit(solution)/shard_map/while/body/eval_jaxpr/ppermute | solution.py:18
  111.5 8.6 %collective-permute-start.1 = (s32[64]{0:T(128)S(1)}, s32[64]{0:T(128)S(1)}, u32[]{:S(2)}, u32[]{:S(2)}) collective-permute-start(s32[64]{0:T(128)S(1)} %get-tuple-element.170), channel_id=1, source_target_pairs={{0,32},{32,64},{64,96},{96,128},{128,160},{160,192},{192,224},{224... | collective-permute-start | bytes 776 | tf_op jit(solution)/shard_map/while/body/eval_jaxpr/ppermute | solution.py:18
  113.5 10.8 %collective-permute-start = (bf16[64,2,256]{2,0,1:T(8,128)(2,1)S(1)}, bf16[64,2,256]{2,0,1:T(8,128)(2,1)S(1)}, u32[]{:S(2)}, u32[]{:S(2)}) collective-permute-start(bf16[64,2,256]{2,0,1:T(8,128)(2,1)S(1)} %get-tuple-element.169), channel_id=1, source_target_pairs={{0,32},{32,64},{64,96},{96,128},{128,160},{160,192},{192,224},{224... | collective-permute-start | bytes 196616 | tf_op jit(solution)/shard_map/while/body/eval_jaxpr/ppermute | solution.py:18
  126.8 8.2 %collective-permute-start.1 = (s32[64]{0:T(128)S(1)}, s32[64]{0:T(128)S(1)}, u32[]{:S(2)}, u32[]{:S(2)}) collective-permute-start(s32[64]{0:T(128)S(1)} %get-tuple-element.170), channel_id=1, source_target_pairs={{0,32},{32,64},{64,96},{96,128},{128,160},{160,192},{192,224},{224... | collective-permute-start | bytes 776 | tf_op jit(solution)/shard_map/while/body/eval_jaxpr/ppermute | solution.py:18
  128.7 8.9 %collective-permute-start = (bf16[64,2,256]{2,0,1:T(8,128)(2,1)S(1)}, bf16[64,2,256]{2,0,1:T(8,128)(2,1)S(1)}, u32[]{:S(2)}, u32[]{:S(2)}) collective-permute-start(bf16[64,2,256]{2,0,1:T(8,128)(2,1)S(1)} %get-tuple-element.169), channel_id=1, source_target_pairs={{0,32},{32,64},{64,96},{96,128},{128,160},{160,192},{192,224},{224... | collective-permute-start | bytes 196616 | tf_op jit(solution)/shard_map/while/body/eval_jaxpr/ppermute | solution.py:18
  140.2 8.2 %collective-permute-start.1 = (s32[64]{0:T(128)S(1)}, s32[64]{0:T(128)S(1)}, u32[]{:S(2)}, u32[]{:S(2)}) collective-permute-start(s32[64]{0:T(128)S(1)} %get-tuple-element.170), channel_id=1, source_target_pairs={{0,32},{32,64},{64,96},{96,128},{128,160},{160,192},{192,224},{224... | collective-permute-start | bytes 776 | tf_op jit(solution)/shard_map/while/body/eval_jaxpr/ppermute | solution.py:18
  142.1 8.9 %collective-permute-start = (bf16[64,2,256]{2,0,1:T(8,128)(2,1)S(1)}, bf16[64,2,256]{2,0,1:T(8,128)(2,1)S(1)}, u32[]{:S(2)}, u32[]{:S(2)}) collective-permute-start(bf16[64,2,256]{2,0,1:T(8,128)(2,1)S(1)} %get-tuple-element.169), channel_id=1, source_target_pairs={{0,32},{32,64},{64,96},{96,128},{128,160},{160,192},{192,224},{224... | collective-permute-start | bytes 196616 | tf_op jit(solution)/shard_map/while/body/eval_jaxpr/ppermute | solution.py:18
  153.6 8.2 %collective-permute-start.1 = (s32[64]{0:T(128)S(1)}, s32[64]{0:T(128)S(1)}, u32[]{:S(2)}, u32[]{:S(2)}) collective-permute-start(s32[64]{0:T(128)S(1)} %get-tuple-element.170), channel_id=1, source_target_pairs={{0,32},{32,64},{64,96},{96,128},{128,160},{160,192},{192,224},{224... | collective-permute-start | bytes 776 | tf_op jit(solution)/shard_map/while/body/eval_jaxpr/ppermute | solution.py:18
  155.5 8.9 %collective-permute-start = (bf16[64,2,256]{2,0,1:T(8,128)(2,1)S(1)}, bf16[64,2,256]{2,0,1:T(8,128)(2,1)S(1)}, u32[]{:S(2)}, u32[]{:S(2)}) collective-permute-start(bf16[64,2,256]{2,0,1:T(8,128)(2,1)S(1)} %get-tuple-element.169), channel_id=1, source_target_pairs={{0,32},{32,64},{64,96},{96,128},{128,160},{160,192},{192,224},{224... | collective-permute-start | bytes 196616 | tf_op jit(solution)/shard_map/while/body/eval_jaxpr/ppermute | solution.py:18
  167.0 8.2 %collective-permute-start.1 = (s32[64]{0:T(128)S(1)}, s32[64]{0:T(128)S(1)}, u32[]{:S(2)}, u32[]{:S(2)}) collective-permute-start(s32[64]{0:T(128)S(1)} %get-tuple-element.170), channel_id=1, source_target_pairs={{0,32},{32,64},{64,96},{96,128},{128,160},{160,192},{192,224},{224... | collective-permute-start | bytes 776 | tf_op jit(solution)/shard_map/while/body/eval_jaxpr/ppermute | solution.py:18
  168.9 8.9 %collective-permute-start = (bf16[64,2,256]{2,0,1:T(8,128)(2,1)S(1)}, bf16[64,2,256]{2,0,1:T(8,128)(2,1)S(1)}, u32[]{:S(2)}, u32[]{:S(2)}) collective-permute-start(bf16[64,2,256]{2,0,1:T(8,128)(2,1)S(1)} %get-tuple-element.169), channel_id=1, source_target_pairs={{0,32},{32,64},{64,96},{96,128},{128,160},{160,192},{192,224},{224... | collective-permute-start | bytes 196616 | tf_op jit(solution)/shard_map/while/body/eval_jaxpr/ppermute | solution.py:18
  180.4 8.5 %collective-permute-start.1 = (s32[64]{0:T(128)S(1)}, s32[64]{0:T(128)S(1)}, u32[]{:S(2)}, u32[]{:S(2)}) collective-permute-start(s32[64]{0:T(128)S(1)} %get-tuple-element.170), channel_id=1, source_target_pairs={{0,32},{32,64},{64,96},{96,128},{128,160},{160,192},{192,224},{224... | collective-permute-start | bytes 776 | tf_op jit(solution)/shard_map/while/body/eval_jaxpr/ppermute | solution.py:18
  182.3 8.9 %collective-permute-start = (bf16[64,2,256]{2,0,1:T(8,128)(2,1)S(1)}, bf16[64,2,256]{2,0,1:T(8,128)(2,1)S(1)}, u32[]{:S(2)}, u32[]{:S(2)}) collective-permute-start(bf16[64,2,256]{2,0,1:T(8,128)(2,1)S(1)} %get-tuple-element.169), channel_id=1, source_target_pairs={{0,32},{32,64},{64,96},{96,128},{128,160},{160,192},{192,224},{224... | collective-permute-start | bytes 196616 | tf_op jit(solution)/shard_map/while/body/eval_jaxpr/ppermute | solution.py:18
  193.8 8.2 %collective-permute-start.1 = (s32[64]{0:T(128)S(1)}, s32[64]{0:T(128)S(1)}, u32[]{:S(2)}, u32[]{:S(2)}) collective-permute-start(s32[64]{0:T(128)S(1)} %get-tuple-element.170), channel_id=1, source_target_pairs={{0,32},{32,64},{64,96},{96,128},{128,160},{160,192},{192,224},{224... | collective-permute-start | bytes 776 | tf_op jit(solution)/shard_map/while/body/eval_jaxpr/ppermute | solution.py:18
  195.7 8.9 %collective-permute-start = (bf16[64,2,256]{2,0,1:T(8,128)(2,1)S(1)}, bf16[64,2,256]{2,0,1:T(8,128)(2,1)S(1)}, u32[]{:S(2)}, u32[]{:S(2)}) collective-permute-start(bf16[64,2,256]{2,0,1:T(8,128)(2,1)S(1)} %get-tuple-element.169), channel_id=1, source_target_pairs={{0,32},{32,64},{64,96},{96,128},{128,160},{160,192},{192,224},{224... | collective-permute-start | bytes 196616 | tf_op jit(solution)/shard_map/while/body/eval_jaxpr/ppermute | solution.py:18
  207.2 8.2 %collective-permute-start.1 = (s32[64]{0:T(128)S(1)}, s32[64]{0:T(128)S(1)}, u32[]{:S(2)}, u32[]{:S(2)}) collective-permute-start(s32[64]{0:T(128)S(1)} %get-tuple-element.170), channel_id=1, source_target_pairs={{0,32},{32,64},{64,96},{96,128},{128,160},{160,192},{192,224},{224... | collective-permute-start | bytes 776 | tf_op jit(solution)/shard_map/while/body/eval_jaxpr/ppermute | solution.py:18
  209.1 9.3 %collective-permute-start = (bf16[64,2,256]{2,0,1:T(8,128)(2,1)S(1)}, bf16[64,2,256]{2,0,1:T(8,128)(2,1)S(1)}, u32[]{:S(2)}, u32[]{:S(2)}) collective-permute-start(bf16[64,2,256]{2,0,1:T(8,128)(2,1)S(1)} %get-tuple-element.169), channel_id=1, source_target_pairs={{0,32},{32,64},{64,96},{96,128},{128,160},{160,192},{192,224},{224... | collective-permute-start | bytes 196616 | tf_op jit(solution)/shard_map/while/body/eval_jaxpr/ppermute | solution.py:18
  220.9 8.2 %collective-permute-start.1 = (s32[64]{0:T(128)S(1)}, s32[64]{0:T(128)S(1)}, u32[]{:S(2)}, u32[]{:S(2)}) collective-permute-start(s32[64]{0:T(128)S(1)} %get-tuple-element.170), channel_id=1, source_target_pairs={{0,32},{32,64},{64,96},{96,128},{128,160},{160,192},{192,224},{224... | collective-permute-start | bytes 776 | tf_op jit(solution)/shard_map/while/body/eval_jaxpr/ppermute | solution.py:18
  222.9 8.9 %collective-permute-start = (bf16[64,2,256]{2,0,1:T(8,128)(2,1)S(1)}, bf16[64,2,256]{2,0,1:T(8,128)(2,1)S(1)}, u32[]{:S(2)}, u32[]{:S(2)}) collective-permute-start(bf16[64,2,256]{2,0,1:T(8,128)(2,1)S(1)} %get-tuple-element.169), channel_id=1, source_target_pairs={{0,32},{32,64},{64,96},{96,128},{128,160},{160,192},{192,224},{224... | collective-permute-start | bytes 196616 | tf_op jit(solution)/shard_map/while/body/eval_jaxpr/ppermute | solution.py:18
  234.3 8.2 %collective-permute-start.1 = (s32[64]{0:T(128)S(1)}, s32[64]{0:T(128)S(1)}, u32[]{:S(2)}, u32[]{:S(2)}) collective-permute-start(s32[64]{0:T(128)S(1)} %get-tuple-element.170), channel_id=1, source_target_pairs={{0,32},{32,64},{64,96},{96,128},{128,160},{160,192},{192,224},{224... | collective-permute-start | bytes 776 | tf_op jit(solution)/shard_map/while/body/eval_jaxpr/ppermute | solution.py:18
  236.3 8.9 %collective-permute-start = (bf16[64,2,256]{2,0,1:T(8,128)(2,1)S(1)}, bf16[64,2,256]{2,0,1:T(8,128)(2,1)S(1)}, u32[]{:S(2)}, u32[]{:S(2)}) collective-permute-start(bf16[64,2,256]{2,0,1:T(8,128)(2,1)S(1)} %get-tuple-element.169), channel_id=1, source_target_pairs={{0,32},{32,64},{64,96},{96,128},{128,160},{160,192},{192,224},{224... | collective-permute-start | bytes 196616 | tf_op jit(solution)/shard_map/while/body/eval_jaxpr/ppermute | solution.py:18
  658.4 25.5 %all-to-all-start.3 = ((bf16[16,8,1,2,1440]{4,3,1,2,0:T(2,128)(2,1)}), bf16[16,8,1,2,1440]{4,3,1,2,0:T(2,128)(2,1)S(1)}, u32[]{:S(2)}, u32[]{:S(2)}) async-start(bf16[16,8,1,2,1440]{4,3,1,2,0:T(2,128)(2,1)} %fusion.23), calls=%async_computation.3 | async-start | bytes 1572864 | tf_op jit(solution)/shard_map/all_to_all | solution.py:55
  (8 other events, 508.4 us)
Sparse Core Ops, SparseCore 0:
  10.5 115.4 all-gather.1
